TPU v7x, 32 devices: a whole 2x2x4 slice. The times are simulated.
32 devices in a mesh: pipe: 2 (over x), dp: 16 (over z, y, core).
Axes of the slice: x: 2, y: 2, z: 4, core: 2. Of those that a mesh axis runs over, the one named last changes fastest.
Arguments:
- acts: bfloat16 [2, 2048, 8192], P('pipe', 'dp'), may hold values from -6 to 6
- incoming: bfloat16 [2, 2048, 8192], P('pipe', 'dp'), may hold values from -6 to 6
- proj_in: bfloat16 [64, 8192], P(None, 'dp'), may hold values from -0.0625 to 0.0625
- proj_out: bfloat16 [64, 8192], P(None, 'dp'), may hold values from -0.0625 to 0.0625
- valid_rows: bfloat16 [2, 128, 4096], P('pipe', 'dp'), may hold values from -0.09375 to 0.09375
- lengths: int32 [16], P('dp'), may hold values from 1 to 128, 1792 in all
- domains: int32 [16], replicated, may hold values from 0 to 15
Outputs:
- domain_gram: float32 [2, 16, 128, 128], P('pipe', 'dp')
All inputs are finite; a program needn't handle non-finite values. No bound on the sum of `lengths` on one device may be relied on, other than what follows from the above.
Results may differ from a plain program's by a relative error of at most 0.004.
Values may be sent and summed in bfloat16 or wider, within the bound.
A program may use at most 128 MiB of HBM per device.

v0:
```python
import jax
import jax.numpy as jnp
from jax import lax
from jax.sharding import PartitionSpec as P

highest_precision = lax.Precision.HIGHEST


def prefix(part, axis, combine, identity):
    count = lax.axis_size(axis)
    place = lax.axis_index(axis)
    ahead = count - 1 - place
    gathered = lax.all_gather(part, axis)
    state = jnp.zeros_like(part) + jnp.asarray(identity, part.dtype)

    def one(lap, state):
        source = count - 1 - lap
        return combine(state, lax.dynamic_index_in_dim(gathered, source, 0, False))

    return lax.fori_loop(0, ahead, one, state)


def add_terms(earlier, later):
    return earlier + later


def body(acts, incoming, proj_in, proj_out, valid_rows, lengths, domains):
    layer_act = acts[0]
    branch = incoming[0]
    rows_here = layer_act.shape[0]
    proj_size = proj_in.shape[0]
    new_act = lax.dot_general(
        layer_act,
        lax.all_gather(proj_in, "dp", axis=1, tiled=True),
        (((1,), (1,)), ((), ())),
        preferred_element_type=jnp.float32,
    )
    new_grad = lax.dot_general(
        branch,
        lax.all_gather(proj_out, "dp", axis=1, tiled=True),
        (((1,), (1,)), ((), ())),
        preferred_element_type=jnp.float32,
    )
    proj_grad = new_grad
    higher = prefix(proj_grad, "pipe", add_terms, jnp.zeros_like(proj_grad))
    proj_grad = higher + proj_grad
    live_count = lengths[0]
    positions = lax.iota(jnp.int32, rows_here)
    weights = jnp.where(positions < live_count, 1.0, 0.0).astype(jnp.float32) / live_count.astype(
        jnp.float32
    )
    scaled = proj_grad * weights[:, None]
    grad_row = lax.dot_general(
        scaled, new_act, (((0,), (0,)), ((), ())), precision=highest_precision
    )
    grad_row = grad_row.reshape(1, proj_size * proj_size).astype(jnp.bfloat16)
    valid_full = lax.all_gather(valid_rows, "dp", axis=1, tiled=True)[0]
    my_index = lax.axis_index("dp")
    scores = lax.dot_general(
        lax.all_gather(grad_row, "dp", axis=0, tiled=True),
        valid_full,
        (((1,), (1,)), ((), ())),
        preferred_element_type=jnp.float32,
    )
    owned = domains == my_index
    kept = scores * owned.astype(jnp.float32)[:, None]
    gram = lax.dot_general(kept, scores, (((0,), (0,)), ((), ())), precision=highest_precision)
    return gram[None, None]


def solution(mesh):
    placed = (
        P("pipe", "dp", None),
        P("pipe", "dp", None),
        P(None, "dp"),
        P(None, "dp"),
        P("pipe", "dp", None),
        P("dp"),
        P(),
    )
    return jax.shard_map(
        body, mesh=mesh, in_specs=placed, out_specs=P("pipe", "dp", None, None), check_vma=False
    )
```

profile of v0, /device:TPU:0, one launch (start us, length us, event | category | flops | bytes accessed | tf_op | source)
XLA Modules:
  0.0 136.5 jit_solution(11406547090230849449)
XLA Ops:
  6.5 0.0 copy-start
  6.5 0.0 all-gather.6.cloned.1.call-start
  6.5 0.7 all-gather.6.cloned.1.call-update
  7.3 0.0 all-gather.8.cloned.1.call-start
  7.3 0.7 all-gather.8.cloned.1.call-update
  8.0 0.0 all-gather.10.cloned.1.call-start
  8.1 0.7 all-gather.10.cloned.1.call-update
  8.7 0.7 compare_convert_fusion
  10.1 38.8 %all-gather.6.cloned.1.call-done = bf16[64,8192]{1,0:T(8,128)(2,1)} async-done(((bf16[64,512]{1,0:T(8,128)(2,1)}), bf16[64,8192]{1,0:T(8,128)(2,1)}) %all-gather.6.cloned.1.call-update) | async-done | bytes 1048592 | tf_op jit(solution)/shard_map/all_gather | solution.py:40
  48.9 0.0 copy-done
  48.9 2.1 %fusion.2 = f32[128,64]{0,1:T(8,128)S(1)} fusion(bf16[64,8192]{1,0:T(8,128)(2,1)} %all-gather.6.cloned.1.call-done, bf16[1,128,8192]{2,1,0:T(8,128)(2,1)S(1)} %copy-done), kind=kOutput, calls=%fused_computation.3 | convolution fusion | flops 134217728 | bytes 3178496 | tf_op jit(solution)/shard_map/dot_general | solution.py:38
  51.0 4.6 %all-gather = f32[256,64]{0,1:T(8,128)S(1)} all-gather(f32[128,64]{0,1:T(8,128)S(1)} %fusion.2), channel_id=2, replica_groups=mesh['pipe'=2,'dp'=16] {'pipe'}, dimensions={0}, use_global_device_ids=true | all-gather | bytes 98304 | tf_op jit(solution)/shard_map/all_gather | solution.py:13
  55.6 0.1 copy.15
  55.7 0.1 while.12
  55.7 0.1 copy.14
  55.8 31.6 %all-gather.8.cloned.1.call-done = bf16[64,8192]{1,0:T(8,128)(2,1)} async-done(((bf16[64,512]{1,0:T(8,128)(2,1)}), bf16[64,8192]{1,0:T(8,128)(2,1)}) %all-gather.8.cloned.1.call-update) | async-done | bytes 1048592 | tf_op jit(solution)/shard_map/all_gather | solution.py:34
  87.3 2.7 %fusion = f32[128,64]{0,1:T(8,128)S(1)} fusion(bf16[64,8192]{1,0:T(8,128)(2,1)} %all-gather.8.cloned.1.call-done, bf16[1,128,8192]{2,1,0:T(8,128)(2,1)} %param.9), kind=kOutput, calls=%fused_computation.1 | convolution fusion | flops 134217728 | bytes 3178496 | tf_op jit(solution)/shard_map/dot_general | solution.py:32
  90.0 0.2 convolution_convert_fusion
  90.2 0.1 reshape.22
  90.3 20.8 %all-gather.1 = bf16[16,1,4096]{2,1,0:T(2,128)(2,1)S(1)} all-gather(bf16[1,1,4096]{2,1,0:T(2,128)(2,1)S(1)} %reshape.22), channel_id=1, replica_groups=mesh['pipe'=2,'dp'=16] {'dp'}, dimensions={0}, use_global_device_ids=true | all-gather | bytes 139264 | tf_op jit(solution)/shard_map/all_gather | solution.py:60
  111.1 16.2 %all-gather.10.cloned.1.call-done = bf16[1,128,4096]{2,1,0:T(8,128)(2,1)} async-done(((bf16[1,8,4096]{2,1,0:T(8,128)(2,1)}), bf16[1,128,4096]{2,1,0:T(8,128)(2,1)}) %all-gather.10.cloned.1.call-update) | async-done | bytes 1048592 | tf_op jit(solution)/shard_map/all_gather | solution.py:57
  127.3 1.6 %fusion.4 = f32[16,128]{1,0:T(8,128)S(1)} fusion(bf16[1,128,4096]{2,1,0:T(8,128)(2,1)} %all-gather.10.cloned.1.call-done, bf16[16,1,4096]{2,1,0:T(2,128)(2,1)S(1)} %all-gather.1), kind=kOutput, calls=%fused_computation.7 | convolution fusion | flops 16777216 | bytes 1187840 | tf_op jit(solution)/shard_map/dot_general | solution.py:59
  128.9 1.0 convolution_bitcast_fusion
  (3 shorter events, 0.0 us)
Async XLA Ops:
  6.5 42.4 %copy-start = (bf16[1,128,8192]{2,1,0:T(8,128)(2,1)S(1)}, bf16[1,128,8192]{2,1,0:T(8,128)(2,1)}, u32[]{:S(2)}) copy-start(bf16[1,128,8192]{2,1,0:T(8,128)(2,1)} %param.10) | copy-start | bytes 6291460
  6.5 42.4 %all-gather.6.cloned.1.call-start = ((), (), s32[]{:S(2)}) async-start(), calls=%async_computation | async-start | bytes 1114112 | tf_op jit(solution)/shard_map/all_gather | solution.py:40
  7.3 80.1 %all-gather.8.cloned.1.call-start = ((), (), s32[]{:S(2)}) async-start(), calls=%async_computation.1 | async-start | bytes 1114112 | tf_op jit(solution)/shard_map/all_gather | solution.py:34
  8.0 119.3 %all-gather.10.cloned.1.call-start = ((), (), s32[]{:S(2)}) async-start(), calls=%async_computation.2 | async-start | bytes 1114112 | tf_op jit(solution)/shard_map/all_gather | solution.py:57
Sparse Core Ops, SparseCore 0:
  9.5 39.3 all-gather.5
  51.0 36.2 all-gather.7
  89.5 37.7 all-gather.9
where the time goes:
time: 137 us; the launch traced here: 136 us
  waiting for transfers between devices  88.7 us (65%)
  blocking collectives  25.4 us (19%)
  between operations  13.8 us (10%)
  matrix products  7.55 us (6%)
    all_gather x1, waiting for transfers between devices, body(): lax.all_gather(proj_out, 'dp', axis=1, tiled=True)  38.8 us
    all_gather x1, waiting for transfers between devices, body(): lax.all_gather(proj_in, 'dp', axis=1, tiled=True)  31.6 us
    all_gather x1, blocking collectives, body(): lax.all_gather(grad_row, 'dp', axis=0, tiled=True)  20.8 us
    all_gather x1, waiting for transfers between devices, body(): valid_full = lax.all_gather(valid_rows, 'dp', axis=1, tiled=True)[0]  16.2 us
    all_gather x1, blocking collectives, prefix(): gathered = lax.all_gather(part, axis)  4.58 us
  transfers between devices with their start and end apart: 3, of which 3 were waited for; matrix products, arithmetic and copies ran while one was open for 4% of the time, Pallas kernels for 0%

commit v1 on v0

v1 whole, which is shorter than its diff:
```python
import functools

import jax
import jax.numpy as jnp
from jax import lax
from jax.experimental import pallas as pl
from jax.experimental.pallas import tpu as pltpu
from jax.sharding import PartitionSpec as P

MESH = pl.DeviceIdType.MESH
HIGHEST = lax.Precision.HIGHEST
CORES = 2
SIDES = 2
GROUP = CORES * SIDES


def kernel(
    stages, dp,
    acts_hbm, inc_hbm, pin_hbm, pout_hbm, valid_hbm, lengths, domains,
    gram_ref,
    acts, inc, pout, pin, valid, valid_full, grad_acc, act_acc, higher, wide, scores, flat, kept,
    load_sem, send_sem, recv_sem, pipe_send, pipe_recv, score_send, score_recv,
):
    stage = lax.axis_index("pipe")
    me = lax.axis_index("dp")
    line_len = dp // GROUP
    line = me // GROUP
    side = (me // CORES) % SIDES
    core = me % CORES
    hbm = (pout_hbm, pin_hbm, valid_hbm.at[0])
    bufs = (pout, pin, valid)

    def at(z, y, c):
        return z * GROUP + y * CORES + c

    loads = [pltpu.make_async_copy(hbm[a], bufs[a].at[me], load_sem.at[a]) for a in range(3)]
    loads.append(pltpu.make_async_copy(inc_hbm.at[0], inc, load_sem.at[3]))
    loads.append(pltpu.make_async_copy(acts_hbm.at[0], acts, load_sem.at[4]))
    for copy in loads:
        copy.start()

    barrier = pltpu.get_barrier_semaphore()
    for k in range(1, dp):
        pl.semaphore_signal(barrier, inc=1, device_id=(stage, (me + k) % dp), device_id_type=MESH)
    for k in range(1, stages):
        pl.semaphore_signal(barrier, inc=1, device_id=((stage + k) % stages, me), device_id_type=MESH)
    grad_acc[...] = jnp.zeros_like(grad_acc)
    act_acc[...] = jnp.zeros_like(act_acc)
    pl.semaphore_wait(barrier, dp + stages - 2)

    up, down, over, across = 0, 1, 2, 3
    targets = (
        at(line + 1, side, core),
        at(line - 1, side, core),
        at(line, 1 - side, core),
        at(line, side, 1 - core),
    )

    def copy_of(a, shard, way):
        return pltpu.make_async_remote_copy(
            src_ref=bufs[a].at[shard],
            dst_ref=bufs[a].at[shard],
            send_sem=send_sem.at[a, way, shard],
            recv_sem=recv_sem.at[a, shard],
            device_id=(stage, targets[way]),
            device_id_type=MESH,
        )

    def arrived(a, shard):
        copy_of(a, shard, across).wait_recv()

    def line_stage(a, d):
        if d == 0:
            loads[a].wait()

            @pl.when(line < line_len - 1)
            def _():
                copy_of(a, me, up).start()

            @pl.when(line > 0)
            def _():
                copy_of(a, me, down).start()

            copy_of(a, me, over).start()
            copy_of(a, me, across).start()
            return
        for way, sign in ((up, -1), (down, 1)):
            source = line + sign * d

            @pl.when((source >= 0) & (source < line_len))
            def _(source=source, way=way):
                shard = at(source, side, core)
                arrived(a, shard)
                more = (line < line_len - 1) if way == up else (line > 0)

                @pl.when(more)
                def _():
                    copy_of(a, shard, way).start()

                copy_of(a, shard, over).start()
                copy_of(a, shard, across).start()

    def sources_of(d):
        if d == 0:
            return [(line, None)]
        return [
            (line + s * d, (line + s * d >= 0) & (line + s * d < line_len)) for s in (-1, 1)
        ]

    def guarded(d, what):
        for source, ok in sources_of(d):
            if ok is None:
                what(source)
            else:
                pl.when(ok)(functools.partial(what, source))

    def side_stage(a, d):
        def one(source):
            shard = at(source, 1 - side, core)
            arrived(a, shard)
            copy_of(a, shard, across).start()

        guarded(d, one)

    def core_stage(a, d):
        def one(source):
            arrived(a, at(source, side, 1 - core))
            arrived(a, at(source, 1 - side, 1 - core))
            base = source * GROUP
            if a == 2:
                rows = valid.shape[1] * GROUP
                part = valid[pl.ds(base, GROUP)].astype(jnp.float32)
                valid_full[pl.ds(pl.multiple_of(source * rows, rows), rows)] = part.reshape(
                    rows, valid.shape[2]
                ).astype(jnp.bfloat16)
                return
            acc, data, buf = (grad_acc, inc, pout) if a == 0 else (act_acc, acts, pin)
            width = buf.shape[2]
            total = acc[...]
            for j in range(GROUP):
                columns = pl.ds(pl.multiple_of((base + j) * width, width), width)
                total += lax.dot_general(
                    buf[base + j], data[:, columns], (((1,), (1,)), ((), ())),
                    preferred_element_type=jnp.float32,
                )
            acc[...] = total

        if d == 0 and a < 2:
            loads[3 + a].wait()
        guarded(d, one)

    def pipe_copy(k):
        return pltpu.make_async_remote_copy(
            src_ref=grad_acc,
            dst_ref=higher.at[k - 1],
            send_sem=pipe_send.at[k - 1],
            recv_sem=pipe_recv.at[k - 1],
            device_id=(stage - k, me),
            device_id_type=MESH,
        )

    steps = [(a, d) for a in range(3) for d in range(line_len)]
    for t in range(len(steps) + 2):
        if t < len(steps):
            line_stage(*steps[t])
        if 1 <= t < len(steps) + 1:
            side_stage(*steps[t - 1])
        if t >= 2:
            core_stage(*steps[t - 2])
            if steps[t - 2] == (0, line_len - 1):
                for k in range(1, stages):
                    @pl.when(stage >= k)
                    def _(k=k):
                        pipe_copy(k).start()

    grad = grad_acc[...]
    for k in range(1, stages):
        @pl.when(stage + k < stages)
        def _(k=k):
            pipe_copy(k).wait_recv()

        grad += jnp.where(stage + k < stages, higher[k - 1], 0.0)
    tokens = grad.shape[1]
    size = grad.shape[0]
    live = lengths[0]
    positions = lax.broadcasted_iota(jnp.int32, (1, tokens), 1)
    weights = jnp.where(positions < live, 1.0, 0.0) / jnp.full(
        (1, tokens), live.astype(jnp.float32), jnp.float32
    )
    scaled = grad * weights
    act = act_acc[...]
    row = lax.dot_general(
        scaled, jnp.concatenate([act, act], axis=0), (((1,), (1,)), ((), ())),
        precision=HIGHEST, preferred_element_type=jnp.float32,
    )
    a_index = lax.broadcasted_iota(jnp.int32, (size, 2 * size), 0)
    half = lax.broadcasted_iota(jnp.int32, (size, 2 * size), 1) // size
    for k in range(size // 2):
        wide[:, 2 * size * k : 2 * size * (k + 1)] = jnp.where(
            a_index == 2 * k + half, row, 0.0
        ).astype(jnp.bfloat16)
    terms = lax.dot_general(
        wide[...], valid_full[...], (((1,), (1,)), ((), ())), preferred_element_type=jnp.float32
    )
    scores[me] = jnp.sum(terms, axis=0, keepdims=True)

    def score_copy(k):
        return pltpu.make_async_remote_copy(
            src_ref=scores.at[me],
            dst_ref=scores.at[me],
            send_sem=score_send.at[k],
            recv_sem=score_recv.at[me],
            device_id=(stage, (me + k) % dp),
            device_id_type=MESH,
        )

    for k in range(1, dp):
        score_copy(k).start()
    for k in range(1, dp):
        peer = (me + k) % dp
        pltpu.make_async_remote_copy(
            src_ref=scores.at[peer],
            dst_ref=scores.at[peer],
            send_sem=score_send.at[k],
            recv_sem=score_recv.at[peer],
            device_id=(stage, peer),
            device_id_type=MESH,
        ).wait_recv()
    for e in range(dp):
        line_e = scores[e]
        flat[e : e + 1, :] = line_e
        kept[e : e + 1, :] = line_e * jnp.where(domains[e] == me, 1.0, 0.0)
    gram_ref[0, 0] = lax.dot_general(
        kept[...], flat[...], (((0,), (0,)), ((), ())), precision=HIGHEST,
        preferred_element_type=jnp.float32,
    )

    for k in range(1, dp):
        score_copy(k).wait_send()
    for k in range(1, stages):
        @pl.when(stage >= k)
        def _(k=k):
            pipe_copy(k).wait_send()

    for a, d in steps:
        def sent(source, a=a, d=d):
            mine = at(source, side, core)
            if d == 0:
                pl.when(line < line_len - 1)(lambda: copy_of(a, mine, up).wait_send())
                pl.when(line > 0)(lambda: copy_of(a, mine, down).wait_send())
            else:
                pl.when((source < line) & (line < line_len - 1))(
                    lambda: copy_of(a, mine, up).wait_send()
                )
                pl.when((source > line) & (line > 0))(lambda: copy_of(a, mine, down).wait_send())
            copy_of(a, mine, over).wait_send()
            copy_of(a, mine, across).wait_send()
            copy_of(a, at(source, 1 - side, core), across).wait_send()

        guarded(d, sent)


def solution(mesh):
    stages, dp = mesh.shape["pipe"], mesh.shape["dp"]

    def body(acts, incoming, proj_in, proj_out, valid_rows, lengths, domains):
        tokens, wide = acts.shape[1:]
        size, shard = proj_in.shape
        held, entries = valid_rows.shape[1:]
        queries = held * dp
        any_spec = pl.BlockSpec(memory_space=pl.ANY)
        smem = pl.BlockSpec(memory_space=pltpu.SMEM)
        f32, bf16 = jnp.float32, jnp.bfloat16
        dma = pltpu.SemaphoreType.DMA
        return pl.pallas_call(
            functools.partial(kernel, stages, dp),
            out_shape=jax.ShapeDtypeStruct((1, 1, queries, queries), f32),
            in_specs=[any_spec] * 5 + [smem] * 2,
            out_specs=pl.BlockSpec(memory_space=pltpu.VMEM),
            scratch_shapes=[
                pltpu.VMEM((tokens, wide), bf16),
                pltpu.VMEM((tokens, wide), bf16),
                pltpu.VMEM((dp, size, shard), bf16),
                pltpu.VMEM((dp, size, shard), bf16),
                pltpu.VMEM((dp, held, entries), bf16),
                pltpu.VMEM((queries, entries), bf16),
                pltpu.VMEM((size, tokens), f32),
                pltpu.VMEM((size, tokens), f32),
                pltpu.VMEM((max(stages - 1, 1), size, tokens), f32),
                pltpu.VMEM((size, entries), bf16),
                pltpu.VMEM((dp, 1, queries), f32),
                pltpu.VMEM((dp, queries), f32),
                pltpu.VMEM((dp, queries), f32),
                dma((5,)),
                dma((3, 4, dp)),
                dma((3, dp)),
                dma((max(stages - 1, 1),)),
                dma((max(stages - 1, 1),)),
                dma((dp,)),
                dma((dp,)),
            ],
            compiler_params=pltpu.CompilerParams(collective_id=0, has_side_effects=True),
        )(acts, incoming, proj_in, proj_out, valid_rows, lengths, domains)

    placed = (
        P("pipe", "dp", None),
        P("pipe", "dp", None),
        P(None, "dp"),
        P(None, "dp"),
        P("pipe", "dp", None),
        P("dp"),
        P(),
    )
    return jax.shard_map(
        body, mesh=mesh, in_specs=placed, out_specs=P("pipe", "dp", None, None), check_vma=False
    )
```

time: 137 us -> 52.9 us (0.39)
  waiting for transfers between devices: 88.7 us -> 0 us
  Pallas kernels: 0 us -> 50.6 us
  blocking collectives: 25.4 us -> 0 us
  between operations: 13.8 us -> 0.66 us
  matrix products: 7.55 us -> 0 us
    all_gather x3 -> x0, waiting for transfers between devices: 86.6 us -> none  [the longest x1 38.8 us: body(): lax.all_gather(proj_out, 'dp', axis=1, tiled=True)]
    pallas_call x0 -> x1, Pallas kernels: none -> 50.6 us  [body(): pl.pallas_call(functools.partial(kernel, stages, dp), out_shape=jax.Shape...]
    all_gather x2 -> x0, blocking collectives: 25.4 us -> none  [the longest x1 20.8 us: body(): lax.all_gather(grad_row, 'dp', axis=0, tiled=True)]
    dot_general x5 -> x0, matrix products: 7.55 us -> none  [the longest x1 2.69 us: body(): lax.dot_general(layer_act, lax.all_gather(proj_in, 'dp', axis=1, tiled=Tr...]
    unnamed x3 -> x0, waiting for transfers between devices: 2.09 us -> none
    unnamed x3 -> x1, local copies, waits for them, and re-layouts: 0.09 us -> 1.47 us
  transfers between devices with their start and end apart: 3 -> 0, of which waited for: 3 -> 0; matrix products, arithmetic and copies ran while one was open for 4% -> 0% of each run, Pallas kernels for 0% -> 0%
where the time goes in v1:
time: 52.9 us; the launch traced here: 52.7 us
  Pallas kernels  50.6 us (96%)
  local copies, waits for them, and re-layouts  1.47 us (3%)
  between operations  0.66 us (1%)
    pallas_call x1, Pallas kernels, body(): pl.pallas_call(functools.partial(kernel, stages, dp), out_shape=jax.Shape...  50.6 us
    unnamed x1, local copies, waits for them, and re-layouts  1.47 us

profile of v1, /device:TPU:0, one launch (start us, length us, event | category | flops | bytes accessed | tf_op | source)
XLA Modules:
  0.0 52.7 jit_solution(15281949917319041174)
XLA Ops:
  0.7 50.6 %shard_map.73 = f32[1,1,128,128]{3,2,1,0:T(8,128)} custom-call(bf16[1,128,8192]{2,1,0:T(8,128)(2,1)} %acts_hbm.1, bf16[1,128,8192]{2,1,0:T(8,128)(2,1)} %inc_hbm.1, bf16[64,512]{1,0:T(8,128)(2,1)} %pin_hbm.1, bf16[64,512]{1,0:T(8,128)(2,1)} %pout_hbm.1, bf16[1,8,4096]{2,1,0:T(8,128)(2,1)} %valid_hbm.1, s32[1]{0:T(128)S(6)} %copy.9.lengths, s32[16]{0:T(128)} %domains.1), custom_call_target="tpu_custom_call" | custom-call | tf_op jit(solution)/shard_map/pallas_call | solution.py:275
  51.2 1.5 %copy.10 = f32[1,1,128,128]{3,2,1,0:T(8,128)} copy(f32[1,1,128,128]{3,2,1,0:T(8,128)} %shard_map.73) | data formatting | bytes 131072

commit v2 on v1

--- a/solution.py
+++ b/solution.py
@@ -12,6 +12,15 @@
 CORES = 2
 SIDES = 2
 GROUP = CORES * SIDES
+REACH = 1
+LINE_STEPS = (1, -1)
+SPLIT = True
+LAGS = (3, 5, 6)
+
+
+def turn(step):
+    a, d = step
+    return 2 * a + d + 1.5 * ((d - 1) // REACH) if d else a - 5
 
 
 def kernel(
@@ -40,65 +49,81 @@
         copy.start()
 
     barrier = pltpu.get_barrier_semaphore()
-    for k in range(1, dp):
-        pl.semaphore_signal(barrier, inc=1, device_id=(stage, (me + k) % dp), device_id_type=MESH)
-    for k in range(1, stages):
-        pl.semaphore_signal(barrier, inc=1, device_id=((stage + k) % stages, me), device_id_type=MESH)
+    heard = jnp.int32(2 + stages - 1)
+    near = [((stage, at(line, 1 - side, core)), None), ((stage, at(line, side, 1 - core)), None)]
+    near += [(((stage + k) % stages, me), None) for k in range(1, stages)]
+    for step in LINE_STEPS:
+        here = line + step
+        near.append(((stage, at(here, side, core)), (here >= 0) & (here < line_len)))
+    for device, ok in near:
+        def greet(device=device):
+            pl.semaphore_signal(barrier, inc=1, device_id=device, device_id_type=MESH)
+
+        if ok is None:
+            greet()
+        else:
+            pl.when(ok)(greet)
+            heard += ok.astype(jnp.int32)
     grad_acc[...] = jnp.zeros_like(grad_acc)
     act_acc[...] = jnp.zeros_like(act_acc)
-    pl.semaphore_wait(barrier, dp + stages - 2)
-
-    up, down, over, across = 0, 1, 2, 3
-    targets = (
-        at(line + 1, side, core),
-        at(line - 1, side, core),
-        at(line, 1 - side, core),
-        at(line, side, 1 - core),
-    )
-
-    def copy_of(a, shard, way):
+    pl.semaphore_wait(barrier, heard)
+
+    over, across, cross = range(len(LINE_STEPS), len(LINE_STEPS) + 3)
+    other_stage = stage + 1 - 2 * (stage % 2)
+    targets = tuple((stage, at(line + step, side, core)) for step in LINE_STEPS) + (
+        (stage, at(line, 1 - side, core)),
+        (stage, at(line, side, 1 - core)),
+        (other_stage, me),
+    )
+
+    def copy_of(a, shard, way, receiving=False):
+        ref = bufs[a].at[shard]
+        if way in (over, cross) and shared(a):
+            half = stage % 2
+            if receiving and way == cross:
+                half = 1 - half
+            rows = bufs[a].shape[1] // 2
+            ref = bufs[a].at[shard, pl.ds(pl.multiple_of(half * rows, rows), rows)]
         return pltpu.make_async_remote_copy(
-            src_ref=bufs[a].at[shard],
-            dst_ref=bufs[a].at[shard],
+            src_ref=ref,
+            dst_ref=ref,
             send_sem=send_sem.at[a, way, shard],
-            recv_sem=recv_sem.at[a, shard],
-            device_id=(stage, targets[way]),
+            recv_sem=recv_sem.at[a, 1 if way == cross else 0, shard],
+            device_id=targets[way],
             device_id_type=MESH,
         )
 
-    def arrived(a, shard):
-        copy_of(a, shard, across).wait_recv()
+    def shared(a):
+        return SPLIT and a < 2 and stages % 2 == 0
+
+    def arrived(a, shard, way=across):
+        copy_of(a, shard, way, True).wait_recv()
+
+    def along_line(a, source, d, act):
+        shard = at(source, side, core)
+        for way, step in enumerate(LINE_STEPS):
+            here = line + step
+            ok = (here >= 0) & (here < line_len)
+            if d:
+                ok = ok & ((source < line) if step > 0 else (source > line))
+
+            @pl.when(ok)
+            def _(way=way):
+                act(copy_of(a, shard, way))
 
     def line_stage(a, d):
         if d == 0:
             loads[a].wait()
-
-            @pl.when(line < line_len - 1)
-            def _():
-                copy_of(a, me, up).start()
-
-            @pl.when(line > 0)
-            def _():
-                copy_of(a, me, down).start()
-
-            copy_of(a, me, over).start()
-            copy_of(a, me, across).start()
-            return
-        for way, sign in ((up, -1), (down, 1)):
-            source = line + sign * d
-
-            @pl.when((source >= 0) & (source < line_len))
-            def _(source=source, way=way):
-                shard = at(source, side, core)
+        def one(source):
+            shard = at(source, side, core)
+            if d:
                 arrived(a, shard)
-                more = (line < line_len - 1) if way == up else (line > 0)
-
-                @pl.when(more)
-                def _():
-                    copy_of(a, shard, way).start()
-
-                copy_of(a, shard, over).start()
-                copy_of(a, shard, across).start()
+            if d % REACH == 0:
+                along_line(a, source, d, lambda copy: copy.start())
+            copy_of(a, shard, over).start()
+            copy_of(a, shard, across).start()
+
+        guarded(d, one)
 
     def sources_of(d):
         if d == 0:
@@ -117,10 +142,19 @@
     def side_stage(a, d):
         def one(source):
             shard = at(source, 1 - side, core)
-            arrived(a, shard)
+            arrived(a, shard, over)
+            copy_of(a, shard, cross if shared(a) else across).start()
+
+        guarded(d, one)
+
+    def cross_stage(a, d):
+        def one(source):
+            shard = at(source, 1 - side, core)
+            arrived(a, shard, cross)
             copy_of(a, shard, across).start()
 
-        guarded(d, one)
+        if shared(a):
+            guarded(d, one)
 
     def core_stage(a, d):
         def one(source):
@@ -160,14 +194,17 @@
         )
 
     steps = [(a, d) for a in range(3) for d in range(line_len)]
-    for t in range(len(steps) + 2):
+    steps.sort(key=turn)
+    for t in range(len(steps) + LAGS[2]):
         if t < len(steps):
             line_stage(*steps[t])
-        if 1 <= t < len(steps) + 1:
-            side_stage(*steps[t - 1])
-        if t >= 2:
-            core_stage(*steps[t - 2])
-            if steps[t - 2] == (0, line_len - 1):
+        if 0 <= t - LAGS[0] < len(steps):
+            side_stage(*steps[t - LAGS[0]])
+        if 0 <= t - LAGS[1] < len(steps):
+            cross_stage(*steps[t - LAGS[1]])
+        if t >= LAGS[2]:
+            core_stage(*steps[t - LAGS[2]])
+            if steps[t - LAGS[2]] == (0, line_len - 1):
                 for k in range(1, stages):
                     @pl.when(stage >= k)
                     def _(k=k):
@@ -245,17 +282,14 @@
     for a, d in steps:
         def sent(source, a=a, d=d):
             mine = at(source, side, core)
-            if d == 0:
-                pl.when(line < line_len - 1)(lambda: copy_of(a, mine, up).wait_send())
-                pl.when(line > 0)(lambda: copy_of(a, mine, down).wait_send())
-            else:
-                pl.when((source < line) & (line < line_len - 1))(
-                    lambda: copy_of(a, mine, up).wait_send()
-                )
-                pl.when((source > line) & (line > 0))(lambda: copy_of(a, mine, down).wait_send())
+            beside = at(source, 1 - side, core)
+            if d % REACH == 0:
+                along_line(a, source, d, lambda copy: copy.wait_send())
             copy_of(a, mine, over).wait_send()
             copy_of(a, mine, across).wait_send()
-            copy_of(a, at(source, 1 - side, core), across).wait_send()
+            if shared(a):
+                copy_of(a, beside, cross).wait_send()
+            copy_of(a, beside, across).wait_send()
 
         guarded(d, sent)
 
@@ -292,8 +326,8 @@
                 pltpu.VMEM((dp, queries), f32),
                 pltpu.VMEM((dp, queries), f32),
                 dma((5,)),
-                dma((3, 4, dp)),
-                dma((3, dp)),
+                dma((3, len(LINE_STEPS) + 3, dp)),
+                dma((3, 2, dp)),
                 dma((max(stages - 1, 1),)),
                 dma((max(stages - 1, 1),)),
                 dma((dp,)),

time: 52.9 us -> 38.5 us (0.73)
  Pallas kernels: 50.6 us -> 36.2 us
    pallas_call x1, Pallas kernels: 50.6 us -> 36.2 us  [body(): pl.pallas_call(functools.partial(kernel, stages, dp), out_shape=jax.Shape...]
where the time goes in v2:
time: 38.5 us; the launch traced here: 38.3 us
  Pallas kernels  36.2 us (94%)
  local copies, waits for them, and re-layouts  1.47 us (4%)
  between operations  0.66 us (2%)
    pallas_call x1, Pallas kernels, body(): pl.pallas_call(functools.partial(kernel, stages, dp), out_shape=jax.Shape...  36.2 us
    unnamed x1, local copies, waits for them, and re-layouts  1.47 us

profile of v2, /device:TPU:0, one launch (start us, length us, event | category | flops | bytes accessed | tf_op | source)
XLA Modules:
  0.0 38.3 jit_solution(6056766305657972287)
XLA Ops:
  0.7 36.2 %shard_map.73 = f32[1,1,128,128]{3,2,1,0:T(8,128)} custom-call(bf16[1,128,8192]{2,1,0:T(8,128)(2,1)} %acts_hbm.1, bf16[1,128,8192]{2,1,0:T(8,128)(2,1)} %inc_hbm.1, bf16[64,512]{1,0:T(8,128)(2,1)} %pin_hbm.1, bf16[64,512]{1,0:T(8,128)(2,1)} %pout_hbm.1, bf16[1,8,4096]{2,1,0:T(8,128)(2,1)} %valid_hbm.1, s32[1]{0:T(128)S(6)} %copy.9.lengths, s32[16]{0:T(128)} %domains.1), custom_call_target="tpu_custom_call" | custom-call | tf_op jit(solution)/shard_map/pallas_call | solution.py:309
  36.9 1.5 %copy.10 = f32[1,1,128,128]{3,2,1,0:T(8,128)} copy(f32[1,1,128,128]{3,2,1,0:T(8,128)} %shard_map.73) | data formatting | bytes 131072

commit v3 on v2

--- a/solution.py
+++ b/solution.py
@@ -14,13 +14,15 @@
 GROUP = CORES * SIDES
 REACH = 1
 LINE_STEPS = (1, -1)
-SPLIT = True
-LAGS = (3, 5, 6)
-
-
-def turn(step):
+SPLIT = (2, 2, 0)
+FIRST, LAP, OVER, CROSS, ACROSS = 2, 3, 4, 4, 3
+
+
+def turn(step, split, kind):
     a, d = step
-    return 2 * a + d + 1.5 * ((d - 1) // REACH) if d else a - 5
+    start = FIRST + a + LAP * (d - 1) if d else a - 9
+    waits = (0, OVER, OVER + (CROSS if split else 0), OVER + (CROSS if split else 0) + ACROSS)
+    return max(start, 0 if kind else -9) + waits[kind]
 
 
 def kernel(
@@ -78,7 +80,7 @@
 
     def copy_of(a, shard, way, receiving=False):
         ref = bufs[a].at[shard]
-        if way in (over, cross) and shared(a):
+        if shared(a) and way != across and (way in (over, cross) or shared(a) == 2):
             half = stage % 2
             if receiving and way == cross:
                 half = 1 - half
@@ -94,7 +96,7 @@
         )
 
     def shared(a):
-        return SPLIT and a < 2 and stages % 2 == 0
+        return SPLIT[a] if stages % 2 == 0 else 0
 
     def arrived(a, shard, way=across):
         copy_of(a, shard, way, True).wait_recv()
@@ -114,14 +116,18 @@
     def line_stage(a, d):
         if d == 0:
             loads[a].wait()
+
         def one(source):
             shard = at(source, side, core)
             if d:
-                arrived(a, shard)
+                arrived(a, shard, 0)
             if d % REACH == 0:
                 along_line(a, source, d, lambda copy: copy.start())
             copy_of(a, shard, over).start()
-            copy_of(a, shard, across).start()
+            if d and shared(a) == 2:
+                copy_of(a, shard, cross).start()
+            else:
+                copy_of(a, shard, across).start()
 
         guarded(d, one)
 
@@ -150,6 +156,9 @@
     def cross_stage(a, d):
         def one(source):
             shard = at(source, 1 - side, core)
+            if d and shared(a) == 2:
+                arrived(a, at(source, side, core), cross)
+                copy_of(a, at(source, side, core), across).start()
             arrived(a, shard, cross)
             copy_of(a, shard, across).start()
 
@@ -194,21 +203,16 @@
         )
 
     steps = [(a, d) for a in range(3) for d in range(line_len)]
-    steps.sort(key=turn)
-    for t in range(len(steps) + LAGS[2]):
-        if t < len(steps):
-            line_stage(*steps[t])
-        if 0 <= t - LAGS[0] < len(steps):
-            side_stage(*steps[t - LAGS[0]])
-        if 0 <= t - LAGS[1] < len(steps):
-            cross_stage(*steps[t - LAGS[1]])
-        if t >= LAGS[2]:
-            core_stage(*steps[t - LAGS[2]])
-            if steps[t - LAGS[2]] == (0, line_len - 1):
-                for k in range(1, stages):
-                    @pl.when(stage >= k)
-                    def _(k=k):
-                        pipe_copy(k).start()
+    events = sorted(
+        (turn(step, shared(step[0]), kind), kind, step) for step in steps for kind in range(4)
+    )
+    for _, kind, step in events:
+        (line_stage, side_stage, cross_stage, core_stage)[kind](*step)
+        if kind == 3 and step == (0, line_len - 1):
+            for k in range(1, stages):
+                @pl.when(stage >= k)
+                def _(k=k):
+                    pipe_copy(k).start()
 
     grad = grad_acc[...]
     for k in range(1, stages):
@@ -289,6 +293,8 @@
             copy_of(a, mine, across).wait_send()
             if shared(a):
                 copy_of(a, beside, cross).wait_send()
+            if d and shared(a) == 2:
+                copy_of(a, mine, cross).wait_send()
             copy_of(a, beside, across).wait_send()
 
         guarded(d, sent)

time: 38.5 us -> 37.2 us (0.966)
  Pallas kernels: 36.2 us -> 34.9 us
    pallas_call x1, Pallas kernels: 36.2 us -> 34.9 us  [body(): pl.pallas_call(functools.partial(kernel, stages, dp), out_shape=jax.Shape...]
where the time goes in v3:
time: 37.2 us; the launch traced here: 37.1 us
  Pallas kernels  34.9 us (94%)
  local copies, waits for them, and re-layouts  1.47 us (4%)
  between operations  0.66 us (2%)
    pallas_call x1, Pallas kernels, body(): pl.pallas_call(functools.partial(kernel, stages, dp), out_shape=jax.Shape...  34.9 us
    unnamed x1, local copies, waits for them, and re-layouts  1.47 us

profile of v3, /device:TPU:0, one launch (start us, length us, event | category | flops | bytes accessed | tf_op | source)
XLA Modules:
  0.0 37.1 jit_solution(5475701563194706570)
XLA Ops:
  0.7 34.9 %shard_map.73 = f32[1,1,128,128]{3,2,1,0:T(8,128)} custom-call(bf16[1,128,8192]{2,1,0:T(8,128)(2,1)} %acts_hbm.1, bf16[1,128,8192]{2,1,0:T(8,128)(2,1)} %inc_hbm.1, bf16[64,512]{1,0:T(8,128)(2,1)} %pin_hbm.1, bf16[64,512]{1,0:T(8,128)(2,1)} %pout_hbm.1, bf16[1,8,4096]{2,1,0:T(8,128)(2,1)} %valid_hbm.1, s32[1]{0:T(128)S(6)} %copy.9.lengths, s32[16]{0:T(128)} %domains.1), custom_call_target="tpu_custom_call" | custom-call | tf_op jit(solution)/shard_map/pallas_call | solution.py:315
  35.6 1.5 %copy.10 = f32[1,1,128,128]{3,2,1,0:T(8,128)} copy(f32[1,1,128,128]{3,2,1,0:T(8,128)} %shard_map.73) | data formatting | bytes 131072
